TPU v7x, 128 devices: a whole 4x4x4 slice. The times are simulated.
128 devices in a mesh: cuts: 8 (over y, core), fsdp: 16 (over z, x).
Axes of the slice: x: 4, y: 4, z: 4, core: 2. Of those that a mesh axis runs over, the one named last changes fastest.
Arguments:
- hidden_states: bfloat16 [65536, 8192], P(('cuts', 'fsdp')), may hold values from -1200 to 1200
- key_cotangent: bfloat16 [65536, 512], P(('cuts', 'fsdp')), may hold values from -60 to 60
- old_weight: bfloat16 [16384, 256], P(('cuts', 'fsdp')), may hold values from -0.0625 to 0.0625
- old_first: bfloat16 [16384, 256], P(('cuts', 'fsdp')), may hold values from -1 to 1
- old_first_scale: float32 [16384], P(('cuts', 'fsdp')), may hold values from 3e-05 to 0.0003
- old_second: bfloat16 [16384, 256], P(('cuts', 'fsdp')), may hold values from 0 to 1
- old_second_scale: float32 [16384], P(('cuts', 'fsdp')), may hold values from 1e-08 to 1e-07
- send_counts: int32 [128, 128], P(('cuts', 'fsdp')), may hold values from 0 to 2, as said below
Outputs:
- input_grad: bfloat16 [65536, 8192], P(('cuts', 'fsdp'))
- new_weight: bfloat16 [8192, 512], P(('cuts', 'fsdp'))
- first_code: bfloat16 [8192, 512], P(('cuts', 'fsdp'))
- first_scale: float32 [8192, 2], P(('cuts', 'fsdp'))
- second_code: bfloat16 [8192, 512], P(('cuts', 'fsdp'))
- second_scale: float32 [8192, 2], P(('cuts', 'fsdp'))
Inputs may be any that keep to these rules, and one draw needn't show every extreme that they name: Every row and every column of send_counts sums to 128; each entry is 0, 1 or 2, and every row and every column holds 2 exactly once.
All inputs are finite; a program needn't handle non-finite values.
Results may differ from a plain program's by a relative error of at most 0.00075.
Values may be sent and summed in bfloat16 or wider, within the bound.
A program may use at most 128 MiB of HBM per device.

v0:
```python
import jax
import jax.numpy as jnp
from jax import lax
from jax.experimental import pallas as pl
from jax.experimental.pallas import tpu as pltpu
from jax.sharding import PartitionSpec as P

STEP = 2000

beta_first = 0.9
beta_second = 0.95
adam_epsilon = 1e-05
learn_rate = 0.001
weight_decay = 0.1
clip_norm = 1.0
tiny_scale = 1e-30

ROWS_OUT = (((0,), (0,)), ((), ()))
AXES = ("cuts", "fsdp")
MESH = pl.DeviceIdType.MESH
ROWS = (88, 88, 80)
FIRST = (0, 88, 176)
ORDER = ((0, 1, 2), (1, 2, 0), (2, 0, 1))
SPLIT = (48, 48, 40)
W_ROWS = (24, 24, 16)
W_FIRST = (0, 24, 48)


def add_into(target, parts):
    outer, inner = target.shape[:2]

    def body(i, carry):
        a, b = i // inner, i % inner
        total = target[a, b]
        for part in parts:
            total = total + part[a, b]
        target[a, b] = total
        return carry

    lax.fori_loop(0, outer * inner, body, 0)


def main_kernel(
    hidden,
    cotangent,
    weight_in,
    first_in,
    second_in,
    first_by_in,
    second_by_in,
    counts_in,
    whole,
    c_own,
    w_out,
    m_out,
    ms_out,
    v_out,
    vs_out,
    h_own,
    h_pair,
    c_pair,
    b0,
    b1,
    b2,
    f0,
    f1,
    f2,
    n0,
    n1,
    n2,
    grad,
    plane,
    line,
    table,
    packed,
    middle,
    arrived,
    owned,
    weight,
    first,
    second,
    first_by,
    second_by,
    counts,
    load_sem,
    pair_send,
    pair_recv,
    ring_send,
    ring_recv,
    sum_send,
    sum_recv,
    deal_send,
    deal_recv,
    line_send,
    line_recv,
    turn_send,
    turn_recv,
    pass_send,
    pass_recv,
):
    cut = lax.axis_index("cuts")
    fs = lax.axis_index("fsdp")
    y, core = cut // 2, cut % 2
    z, x = fs // 4, fs % 4
    here = (y, z, x)

    def at(y, z, x, core):
        return (y * 2 + core, z * 4 + x)

    def neighbour(axis, step):
        place = list(here)
        place[axis] = (place[axis] + step) % 4
        return at(*place, core)

    partner = at(y, z, x, 1 - core)

    order = [(y + s) % 4 for s in (2, 1, 3, 0)]
    state = [
        pltpu.make_async_copy(a, b, load_sem.at[5 + n])
        for n, (a, b) in enumerate(
            (
                (weight_in, weight),
                (first_in, first),
                (second_in, second),
                (first_by_in, first_by),
                (second_by_in, second_by),
                (counts_in, counts),
            )
        )
    ]
    for copy in state:
        copy.start()
    loads = [pltpu.make_async_copy(cotangent, c_own, load_sem.at[4])]
    loads[0].start()
    for i, yy in enumerate(order):
        cols = pl.multiple_of(yy * 2048 + core * 1024, 1024)
        copy = pltpu.make_async_copy(hidden.at[:, pl.ds(cols, 1024)], h_own.at[i], load_sem.at[i])
        copy.start()
        loads.append(copy)

    f32, b16 = jnp.float32, jnp.bfloat16
    barrier = pltpu.get_barrier_semaphore()

    for s in range(1, 16):
        pl.semaphore_signal(barrier, inc=1, device_id=(cut, (fs + s) % 16), device_id_type=MESH)
    for s in range(1, 8):
        pl.semaphore_signal(barrier, inc=1, device_id=((cut + s) % 8, fs), device_id_type=MESH)

    row = lax.broadcasted_iota(jnp.int32, (128, 128), 0)
    col = lax.broadcasted_iota(jnp.int32, (128, 128), 1)
    for copy in state:
        copy.wait()
    mine = counts[...]
    starts = jnp.sum(jnp.where(col < row, mine, 0).astype(f32), axis=1, keepdims=True)
    amount = jnp.sum(jnp.where(col == row, mine, 0).astype(f32), axis=1, keepdims=True)
    slot = col.astype(f32)
    values = jnp.concatenate([weight[...], first[...], second[...]], axis=1)
    table[...] = jnp.zeros_like(table)
    for place in range(2):
        pick = (slot == starts + place) & (amount > place)
        chosen = jnp.dot(
            jnp.where(pick, 1.0, 0.0).astype(b16), values, preferred_element_type=f32
        )
        for q in range(6):
            table[pl.ds(place * 8 + q, 128, stride=16), :] = chosen[:, q * 128 : q * 128 + 128]
        side = jnp.where((col == 6) & (amount > place), 1.0, 0.0)
        for n, by in enumerate((first_by, second_by)):
            rest = jnp.sum(jnp.where(pick, by[...], 0.0), axis=1, keepdims=True)
            for part in range(3):
                high = rest.astype(b16).astype(f32)
                side = side + jnp.where(col == n * 3 + part, high, 0.0)
                rest = rest - high
        table[pl.ds(place * 8 + 6, 128, stride=16), :] = side
    packed[...] = table[...].astype(b16).reshape(8, 16, 16, 128)
    middle[:, fs] = packed[:, fs]

    def own_part(i):
        loads[1 + i].wait()
        spread(i, lax.dot_general(h_own[i], c_own[...], ROWS_OUT, preferred_element_type=f32), False)

    def pair_part(i):
        pairs[1 + i].wait_recv()
        spread(i, lax.dot_general(h_pair[i], c_pair[...], ROWS_OUT, preferred_element_type=f32), True)

    def spread(i, total, more):
        yy = order[i]
        for zz in range(4):
            for xx in range(4):
                part = total[zz * 256 + xx * 64 : zz * 256 + xx * 64 + 64]
                for buf, place, low, value in (
                    (b0, (yy, zz, xx), 0, part[:, 0:128]),
                    (b0, (yy, zz, xx), 64, part[0:24, 128:256]),
                    (b1, (zz, xx, yy), 0, part[24:64, 128:256]),
                    (b1, (zz, xx, yy), 40, part[0:48, 256:384]),
                    (b2, (xx, yy, zz), 0, part[48:64, 256:384]),
                    (b2, (xx, yy, zz), 16, part[:, 384:512]),
                ):
                    at = place + (slice(low, low + value.shape[0]),)
                    buf[at] = buf[at] + value if more else value

    loads[0].wait()
    own_part(0)
    own_part(1)
    pl.semaphore_wait(barrier, 22)

    def remote(src, dst, send, recv, device):
        return pltpu.make_async_remote_copy(
            src_ref=src,
            dst_ref=dst,
            send_sem=send,
            recv_sem=recv,
            device_id=device,
            device_id_type=MESH,
        )

    for s in range(1, 16):
        other = (fs + s) % 16
        remote(
            packed.at[:, other], middle.at[:, fs], deal_send, deal_recv, (cut, other)
        ).start()
    dealt = remote(
        packed.at[:, pl.ds(0, 15)], middle.at[:, pl.ds(0, 15)], deal_send, deal_recv, partner
    )

    pairs = [remote(cotangent, c_pair, pair_send.at[4], pair_recv.at[4], partner)]
    pairs[0].start()
    for i, yy in enumerate(order):
        cols = pl.multiple_of(yy * 2048 + (1 - core) * 1024, 1024)
        copy = remote(
            hidden.at[:, pl.ds(cols, 1024)],
            h_pair.at[i],
            pair_send.at[i],
            pair_recv.at[i],
            partner,
        )
        copy.start()
        pairs.append(copy)

    bufs, fars, nears = (b0, b1, b2), (f0, f1, f2), (n0, n1, n2)

    class Stage:
        def __init__(self, colour, phase):
            self.axis = ORDER[colour][phase]
            self.mine = here[self.axis]
            index = tuple(here[a] for a in ORDER[colour][:phase])
            self.buf = bufs[colour].at[index] if phase else bufs[colour]
            self.phase = phase
            rows = ROWS[colour]
            if phase == 0:
                self.halves = ((pl.ds(0, 2),), (pl.ds(2, 2),))
            elif phase == 1:
                self.halves = ((pl.ds(0, 2),), (pl.ds(2, 2),))
            else:
                cut_at = SPLIT[colour]
                self.halves = ((pl.ds(0, cut_at),), (pl.ds(cut_at, rows - cut_at),))
            self.far = [fars[colour][phase].at[d] for d in range(2)]
            if phase == 2:
                self.far = [fars[colour][phase].at[d, h[0]] for d, h in enumerate(self.halves)]
            self.near = [nears[colour][phase].at[d] for d in range(2)]
            base = (colour * 3 + phase) * 6
            self.copies = []
            for d, step in enumerate((1, -1)):
                to = neighbour(self.axis, step)
                far = self.buf.at[((self.mine + 2) % 4,) + self.halves[d]]
                close = (self.mine + step) % 4
                own = self.buf.at[(close,) + self.halves[1 - d]]
                acc = self.buf.at[(close,) + self.halves[d]]
                self.copies.append(
                    (
                        remote(far, self.far[d], ring_send.at[base + d], ring_recv.at[base + d], to),
                        remote(
                            own,
                            self.near[d].at[self.halves[1 - d]],
                            ring_send.at[base + 2 + d],
                            ring_recv.at[base + 2 + d],
                            to,
                        ),
                        remote(
                            acc,
                            self.near[d].at[self.halves[d]],
                            ring_send.at[base + 4 + d],
                            ring_recv.at[base + 4 + d],
                            to,
                        ),
                        acc,
                    )
                )

        def add(self, target, parts):
            if self.phase == 0:
                add_into(target, parts)
            elif self.phase == 1:
                for i in range(target.shape[0]):
                    total = target[i]
                    for part in parts:
                        total = total + part[i]
                    target[i] = total
            else:
                total = target[...]
                for part in parts:
                    total = total + part[...]
                target[...] = total

        def far_out(self):
            for d in range(2):
                self.copies[d][0].start()

        def own_out(self):
            for d in range(2):
                self.copies[d][1].start()

        def middle(self):
            for d in range(2):
                far, _, onward, acc = self.copies[d]
                far.wait_recv()
                self.add(acc, [self.far[d]])
                onward.start()

        def finish(self):
            for d in range(2):
                self.copies[d][1].wait_recv()
                self.copies[d][2].wait_recv()
            self.add(self.buf.at[self.mine], self.near)

        def drain(self):
            for d in range(2):
                for c in range(3):
                    self.copies[d][c].wait_send()

    class Turn:
        def __init__(self, colour, phase):
            self.colour, self.phase = colour, phase
            self.axis = ORDER[colour][phase]
            self.mine = here[self.axis]
            pieces = range(4) if phase == 2 else (None,)
            base = (0, 12, 24)[phase] + colour * (12 if phase == 2 else 4)
            self.begun, self.onward = ([], []), ([], [])
            for d, step in enumerate((1, -1)):
                to = neighbour(self.axis, step)
                for piece in pieces if d == 0 or phase < 2 else (2, 3, 0, 1):
                    own = self.region(self.mine, piece=piece)
                    self.begun[d].append(
                        remote(own, own, turn_send.at[base], turn_recv.at[base], to)
                    )
                    base += 1
                for piece in ((0, 1), (2, 3))[d] if phase == 2 else (None,):
                    other = self.region((self.mine - step) % 4, d if phase < 2 else None, piece)
                    self.onward[d].append(
                        remote(other, other, turn_send.at[base], turn_recv.at[base], to)
                    )
                    base += 1

        def region(self, index, half=None, piece=None):
            place = list(here)
            for a in ORDER[self.colour][: self.phase]:
                place[a] = pl.ds(0, 4)
            place[self.axis] = index
            cols = pl.ds(0, 512)
            if half is not None and self.phase == 0:
                cols = pl.ds(half * 256, 256)
            elif half is not None:
                place[ORDER[self.colour][0]] = pl.ds(half * 2, 2)
            if piece is not None:
                place[ORDER[self.colour][0]] = piece
            rows = pl.ds(W_FIRST[self.colour], W_ROWS[self.colour])
            return whole.at[place[0], core, place[1], place[2], rows, cols]

        def begin(self, n=0):
            for d in range(2):
                self.begun[d][n].start()

        def middle(self, n=0):
            for d in range(2):
                self.begun[d][n].wait_recv()
                self.onward[d][n].start()

        def arrive(self, n):
            for d in range(2):
                self.begun[d][n].wait_recv()

        def finish(self, n=0):
            for d in range(2):
                self.onward[d][n].wait_recv()

        def drain(self):
            for d in range(2):
                for c in self.begun[d] + self.onward[d]:
                    c.wait_send()

    def hand(turn, index, n):
        slab = turn.region(index)
        k = turn.colour * 4 + n
        return remote(slab, slab, pass_send.at[k], pass_recv.at[k], partner)

    stages = [[Stage(colour, phase) for colour in range(3)] for phase in range(3)]
    turns = [[Turn(colour, phase) for colour in range(3)] for phase in range(3)]

    def each(things, step, *given):
        for thing in things:
            getattr(thing, step)(*given)

    def unpack():
        lined.wait_recv()
        table[...] = arrived[...].reshape(2048, 128).astype(f32)
        marks, before = [], 0.0
        for place in range(2):
            mark = table[pl.ds(place * 8 + 6, 128, stride=16), :][:, 6:7]
            marks.append(jnp.sum(jnp.where(row == col, mark, 0.0), axis=0, keepdims=True))
            before = before + jnp.sum(jnp.where(row < col, mark, 0.0), axis=0, keepdims=True)
        target = jnp.concatenate([before, before + marks[0]], axis=1)
        mark = jnp.concatenate(marks, axis=1)
        blocks = jnp.concatenate(
            [
                jnp.concatenate(
                    [table[pl.ds(place * 8 + q, 128, stride=16), :].astype(b16) for q in range(7)],
                    axis=1,
                )
                for place in range(2)
            ],
            axis=0,
        )
        new_row = lax.broadcasted_iota(jnp.int32, (64, 256), 0).astype(f32)
        for h in range(2):
            choose = (target == 2.0 * new_row + h) & (mark > 0.5)
            owned[h] = jnp.dot(
                jnp.where(choose, 1.0, 0.0).astype(b16), blocks, preferred_element_type=f32
            )
            whole[y, core, z, x, :, h * 256 : h * 256 + 256] = owned[h, :, 0:256].astype(b16)


    own_part(2)
    own_part(3)
    dealt.wait_recv()
    arrived[cut] = middle[cut]
    for s in range(1, 8):
        other = (cut + s) % 8
        remote(middle.at[other], arrived.at[cut], line_send, line_recv, (other, fs)).start()
    lined = remote(
        middle.at[pl.ds(0, 7)], arrived.at[pl.ds(0, 7)], line_send, line_recv, partner
    )
    pairs[0].wait_recv()
    pair_part(0)
    each(stages[0][:1], "far_out")
    pair_part(1)
    pair_part(2)
    pair_part(3)
    each(stages[0][1:], "far_out")
    unpack()
    each(turns[0], "begin")
    each(stages[0], "own_out")
    each(turns[0], "middle")
    each(stages[0], "middle")
    each(turns[0], "finish")
    each(turns[1], "begin")
    each(stages[0], "finish")
    each(stages[1], "far_out")
    each(stages[1], "own_out")
    each(turns[1], "middle")
    each(stages[1], "middle")
    each(turns[1], "finish")
    each(turns[2], "begin", 0)
    passes = [hand(t, t.mine, 0) for t in turns[2]]
    for p in passes:
        p.start()
    each(stages[1], "finish")
    each(stages[2], "far_out")
    each(stages[2], "own_out")
    each(turns[2], "begin", 1)
    each(turns[2], "middle", 0)
    each(stages[2], "middle")
    each(turns[2], "begin", 2)
    each(stages[2], "finish")

    for colour in range(3):
        index = tuple(here[a] for a in ORDER[colour])
        grad[FIRST[colour] : FIRST[colour] + ROWS[colour], :] = bufs[colour][index] * (1.0 / 65536)

    g = grad[...]
    squares = jnp.sum((g * g).reshape(32, 8, 128), axis=0)

    def tell(board, mine, count, base, target):
        copies = [
            remote(
                board.at[mine], board.at[mine], sum_send.at[base + s], sum_recv.at[base + s], target(s)
            )
            for s in range(1, count)
        ]
        for c in copies:
            c.start()
        return copies

    def hear(board, count, copies):
        for c in copies:
            c.wait()
        total = board[0]
        for s in range(1, count):
            total = total + board[s]
        return total

    plane[fs] = squares
    told = tell(plane, fs, 16, 0, lambda s: (cut, (fs + s) % 16))
    each(turns[2], "begin", 3)
    each(turns[2], "middle", 1)
    for t in turns[2]:
        t.arrive(2)
        t.arrive(3)
        for n, step in ((1, -1), (2, 1)):
            p = hand(t, (t.mine + step) % 4, n)
            p.start()
            passes.append(p)
    squares = hear(plane, 16, told)
    line[cut] = squares
    told = tell(line, cut, 8, 16, lambda s: ((cut + s) % 8, fs))
    for t in turns[2]:
        t.finish(0)
        t.finish(1)
        p = hand(t, (t.mine + 2) % 4, 3)
        p.start()
        passes.append(p)
    squares = hear(line, 8, told)
    norm = jnp.sqrt(jnp.sum(squares, keepdims=True))
    factor = jnp.minimum(1.0, clip_norm / (norm + 1e-06))

    eye = lax.broadcasted_iota(jnp.int32, (64, 64), 0) == lax.broadcasted_iota(
        jnp.int32, (64, 64), 1
    )
    for h in range(2):
        m_new, v_new = [], []
        m_by = owned[h, :, 768:769] + owned[h, :, 769:770] + owned[h, :, 770:771]
        v_by = owned[h, :, 771:772] + owned[h, :, 772:773] + owned[h, :, 773:774]
        for n in range(2):
            j = 2 * h + n
            cols = slice(j * 128, j * 128 + 128)
            clipped = grad[j * 64 : j * 64 + 64, :] * factor
            m_old = owned[h, :, 256 + n * 128 : 384 + n * 128] * m_by
            v_old = owned[h, :, 512 + n * 128 : 640 + n * 128] * v_by
            m = beta_first * m_old + (1.0 - beta_first) * clipped
            v = beta_second * v_old + (1.0 - beta_second) * clipped * clipped
            m_hat = m / (1.0 - beta_first**STEP)
            v_hat = v / (1.0 - beta_second**STEP)
            w_old = owned[h, :, n * 128 : n * 128 + 128]
            w_out[:, cols] = (
                w_old
                - learn_rate * (m_hat / (jnp.sqrt(v_hat) + adam_epsilon) + weight_decay * w_old)
            ).astype(b16)
            m_new.append(m)
            v_new.append(v)
        m_scale = (
            jnp.max(jnp.maximum(jnp.abs(m_new[0]), jnp.abs(m_new[1])), axis=1, keepdims=True)
            + tiny_scale
        )
        v_scale = jnp.max(jnp.maximum(v_new[0], v_new[1]), axis=1, keepdims=True) + tiny_scale
        ms_out[h : h + 1, :] = jnp.sum(jnp.where(eye, m_scale, 0.0), axis=0, keepdims=True)
        vs_out[h : h + 1, :] = jnp.sum(jnp.where(eye, v_scale, 0.0), axis=0, keepdims=True)
        for n in range(2):
            cols = slice((2 * h + n) * 128, (2 * h + n) * 128 + 128)
            m_out[:, cols] = (m_new[n] / m_scale).astype(b16)
            v_out[:, cols] = (v_new[n] / v_scale).astype(b16)

    for p in passes:
        p.wait()
    for c in pairs:
        c.wait_send()
    lined.wait_send()
    dealt.wait_send()
    for group in stages + turns:
        each(group, "drain")


def main_call(*given):
    vmem = pl.BlockSpec(memory_space=pltpu.VMEM)
    hbm = pl.BlockSpec(memory_space=pltpu.HBM)
    f32, b16 = jnp.float32, jnp.bfloat16
    scratch = [
        pltpu.VMEM((4, 512, 1024), b16),
        pltpu.VMEM((4, 512, 1024), b16),
        pltpu.VMEM((512, 512), b16),
    ]
    scratch += [pltpu.VMEM((4, 4, 4, r, 128), f32) for r in ROWS]
    scratch += [
        [
            pltpu.VMEM((2, 2, 4, r, 128), f32),
            pltpu.VMEM((2, 2, r, 128), f32),
            pltpu.VMEM((2, r, 128), f32),
        ]
        for r in ROWS
    ]
    scratch += [
        [
            pltpu.VMEM((2, 4, 4, r, 128), f32),
            pltpu.VMEM((2, 4, r, 128), f32),
            pltpu.VMEM((2, r, 128), f32),
        ]
        for r in ROWS
    ]
    scratch += [
        pltpu.VMEM((256, 128), f32),
        pltpu.VMEM((16, 8, 128), f32),
        pltpu.VMEM((8, 8, 128), f32),
        pltpu.VMEM((2048, 128), f32),
        pltpu.VMEM((8, 16, 16, 128), b16),
        pltpu.VMEM((8, 16, 16, 128), b16),
        pltpu.VMEM((8, 16, 16, 128), b16),
        pltpu.VMEM((2, 64, 896), f32),
        pltpu.VMEM((128, 256), b16),
        pltpu.VMEM((128, 256), b16),
        pltpu.VMEM((128, 256), b16),
        pltpu.VMEM((1, 128), f32),
        pltpu.VMEM((1, 128), f32),
        pltpu.VMEM((1, 128), jnp.int32),
        pltpu.SemaphoreType.DMA((11,)),
        pltpu.SemaphoreType.DMA((5,)),
        pltpu.SemaphoreType.DMA((5,)),
        pltpu.SemaphoreType.DMA((54,)),
        pltpu.SemaphoreType.DMA((54,)),
        pltpu.SemaphoreType.DMA((24,)),
        pltpu.SemaphoreType.DMA((24,)),
        pltpu.SemaphoreType.DMA,
        pltpu.SemaphoreType.DMA,
        pltpu.SemaphoreType.DMA,
        pltpu.SemaphoreType.DMA,
        pltpu.SemaphoreType.DMA((60,)),
        pltpu.SemaphoreType.DMA((60,)),
        pltpu.SemaphoreType.DMA((12,)),
        pltpu.SemaphoreType.DMA((12,)),
    ]
    return pl.pallas_call(
        main_kernel,
        out_shape=(
            pltpu.VMEM((4, 2, 4, 4, 64, 512), b16),
            pltpu.VMEM((512, 512), b16),
            pltpu.VMEM((64, 512), b16),
            pltpu.VMEM((64, 512), b16),
            pltpu.VMEM((2, 64), f32),
            pltpu.VMEM((64, 512), b16),
            pltpu.VMEM((2, 64), f32),
        ),
        in_specs=[hbm] * 8,
        out_specs=(vmem,) * 7,
        scratch_shapes=scratch,
        compiler_params=pltpu.CompilerParams(
            collective_id=0, has_side_effects=True, vmem_limit_bytes=57_400_000
        ),
        name="exchange_adam",
    )(*given)


def last_kernel(cotangent, weight, *refs):
    given, (out, *kept), (slab, sems) = refs[:5], refs[5:11], refs[11:]
    copies = []
    for y in range(4):
        for core in range(2):
            i = y * 2 + core
            slab[i] = lax.dot_general(
                cotangent[...],
                weight[y, core].reshape(1024, 512),
                (((1,), (1,)), ((), ())),
                preferred_element_type=jnp.float32,
            ).astype(jnp.bfloat16)
            copies.append(
                pltpu.make_async_copy(
                    slab.at[i], out.at[:, pl.ds(i * 1024, 1024)], sems.at[i]
                )
            )
            copies[-1].start()
    for a, b in zip(given, kept):
        b[...] = a[...]
    for c in copies:
        c.wait()


def last_call(cotangent, weight, small):
    vmem = pl.BlockSpec(memory_space=pltpu.VMEM)
    held = [pltpu.with_memory_space_constraint(a, pltpu.VMEM) for a in (cotangent, weight, *small)]
    return pl.pallas_call(
        last_kernel,
        out_shape=[jax.ShapeDtypeStruct((512, 8192), jnp.bfloat16)]
        + [jax.ShapeDtypeStruct(a.shape, a.dtype) for a in small],
        in_specs=[vmem] * 7,
        out_specs=[pl.BlockSpec(memory_space=pl.ANY)] + [vmem] * 5,
        scratch_shapes=[pltpu.VMEM((8, 512, 1024), jnp.bfloat16), pltpu.SemaphoreType.DMA((8,))],
        compiler_params=pltpu.CompilerParams(vmem_limit_bytes=24_000_000),
        name="input_grad",
    )(*held)


def shards(
    hidden_states,
    key_cotangent,
    old_weight,
    old_first,
    old_first_scale,
    old_second,
    old_second_scale,
    send_counts,
):
    gathered, cotangent, *small = main_call(
        hidden_states, key_cotangent, old_weight, old_first, old_second,
        old_first_scale[None], old_second_scale[None], send_counts,
    )
    input_grad, w_new, m_code, m_scale, v_code, v_scale = last_call(
        cotangent, gathered, small
    )
    return (input_grad, w_new, m_code, m_scale.T, v_code, v_scale.T)


def solution(mesh):
    rows = P(AXES, None)
    placed = (rows, rows, rows, rows, P(AXES), rows, P(AXES), rows)
    return jax.shard_map(
        shards, mesh=mesh, in_specs=placed, out_specs=(rows,) * 6, check_vma=False
    )
```

profile of v0, /device:TPU:1, one launch (start us, length us, event | category | flops | bytes accessed | tf_op | source)
XLA Modules:
  0.0 88.8 jit_solution(17234385278086495435)
XLA Ops:
  0.6 81.7 %exchange_adam.1 = (bf16[4,2,4,4,64,512]{5,4,3,2,1,0:T(8,128)(2,1)S(1)}, bf16[512,512]{1,0:T(8,128)(2,1)S(1)}, bf16[64,512]{1,0:T(8,128)(2,1)S(1)}, bf16[64,512]...) custom-call(bf16[512,8192]{1,0:T(8,128)(2,1)} %hidden.1, ...), custom_call_target="tpu_custom_call" | custom-call | tf_op jit(solution)/shard_map/exchange_adam/pallas_call | solution.py:627
  82.4 6.3 %input_grad.1 = (bf16[512,8192]{1,0:T(8,128)(2,1)}, bf16[64,512]{1,0:T(8,128)(2,1)}, bf16[64,512]{1,0:T(8,128)(2,1)}, f32[2,64]{1,0:T(2,128)}, bf16[64,512]{1,0:T(8,128)(2,1)}, /*index=5*/f32[2,64]{1,0:T(2,128)}) custom-call(bf16[512,512]{1,0:T(8,128)(2,1)S(1)} %get-tuple-element.19.cotangent, bf16[4,2,4,4,64,512]{5,4,3,2,1,0:T(8,128)(2,1)S(1)} %get-tuple-element.20.weight, ...), custom_call_target="tpu_custom_call" | custom-call | tf_op jit(solution)/shard_map/input_grad/pallas_call | solution.py:675
where the time goes:
time: 88.9 us; the launch traced here: 88.8 us
  Pallas kernels  88 us (99%)
    pallas_call x1, Pallas kernels, main_call(): pl.pallas_call(main_kernel, out_shape=(pltpu.VMEM((4, 2, 4, 4, 64, 512),...  81.7 us
    pallas_call x1, Pallas kernels, last_call(): pl.pallas_call(last_kernel, out_shape=[jax.ShapeDtypeStruct((512, 8192),...  6.28 us

commit v1 on v0

--- a/solution.py
+++ b/solution.py
@@ -75,6 +75,9 @@
     packed,
     middle,
     arrived,
+    second_out,
+    second_mid,
+    second_last,
     owned,
     weight,
     first,
@@ -87,12 +90,18 @@
     pair_recv,
     ring_send,
     ring_recv,
+    far_send,
+    far_recv,
     sum_send,
     sum_recv,
     deal_send,
     deal_recv,
     line_send,
     line_recv,
+    extra_send,
+    extra_recv,
+    extra_line_send,
+    extra_line_recv,
     turn_send,
     turn_recv,
     pass_send,
@@ -156,23 +165,37 @@
     slot = col.astype(f32)
     values = jnp.concatenate([weight[...], first[...], second[...]], axis=1)
     table[...] = jnp.zeros_like(table)
-    for place in range(2):
-        pick = (slot == starts + place) & (amount > place)
-        chosen = jnp.dot(
-            jnp.where(pick, 1.0, 0.0).astype(b16), values, preferred_element_type=f32
-        )
-        for q in range(6):
-            table[pl.ds(place * 8 + q, 128, stride=16), :] = chosen[:, q * 128 : q * 128 + 128]
-        side = jnp.where((col == 6) & (amount > place), 1.0, 0.0)
+
+    def sided(pick, rows, seven):
+        side = jnp.where(rows == 6, 1.0, 0.0) * jnp.sum(pick, axis=1, keepdims=True)
+        side = side + jnp.where(rows == 7, seven, 0.0)
         for n, by in enumerate((first_by, second_by)):
-            rest = jnp.sum(jnp.where(pick, by[...], 0.0), axis=1, keepdims=True)
+            rest = jnp.sum(pick * by[...], axis=1, keepdims=True)
             for part in range(3):
                 high = rest.astype(b16).astype(f32)
-                side = side + jnp.where(col == n * 3 + part, high, 0.0)
+                side = side + jnp.where(rows == n * 3 + part, high, 0.0)
                 rest = rest - high
-        table[pl.ds(place * 8 + 6, 128, stride=16), :] = side
-    packed[...] = table[...].astype(b16).reshape(8, 16, 16, 128)
+        return side
+
+    pick = jnp.where((slot == starts) & (amount > 0), 1.0, 0.0)
+    chosen = jnp.dot(pick.astype(b16), values, preferred_element_type=f32)
+    for q in range(6):
+        table[pl.ds(q, 128, stride=8), :] = chosen[:, q * 128 : q * 128 + 128]
+    table[pl.ds(6, 128, stride=8), :] = sided(pick, col, amount)
+    packed[...] = table[...].astype(b16).reshape(8, 16, 8, 128)
     middle[:, fs] = packed[:, fs]
+    twice = amount > 1
+    pick = jnp.sum(jnp.where(twice & (slot == starts + 1), 1.0, 0.0), axis=0, keepdims=True)
+    owner = jnp.sum(
+        jnp.where(twice, row[:, 0:1].astype(f32), 0.0), axis=0, keepdims=True
+    )
+    pick = jnp.broadcast_to(pick, (8, 128))
+    chosen = jnp.dot(pick.astype(b16), values, preferred_element_type=f32)
+    eight = row[0:8]
+    extra = jnp.where(eight == 6, sided(pick, col[0:8], owner), 0.0)
+    for q in range(6):
+        extra = extra + jnp.where(eight == q, chosen[:, q * 128 : q * 128 + 128], 0.0)
+    second_out[fs] = extra.astype(b16)
 
     def own_part(i):
         loads[1 + i].wait()
@@ -218,8 +241,14 @@
         remote(
             packed.at[:, other], middle.at[:, fs], deal_send, deal_recv, (cut, other)
         ).start()
+        remote(
+            second_out.at[fs], second_out.at[fs], extra_send, extra_recv, (cut, other)
+        ).start()
     dealt = remote(
         packed.at[:, pl.ds(0, 15)], middle.at[:, pl.ds(0, 15)], deal_send, deal_recv, partner
+    )
+    seconds = remote(
+        second_out.at[pl.ds(0, 15)], second_out.at[pl.ds(0, 15)], extra_send, extra_recv, partner
     )
 
     pairs = [remote(cotangent, c_pair, pair_send.at[4], pair_recv.at[4], partner)]
@@ -286,6 +315,34 @@
                     )
                 )
 
+            self.split = []
+            if phase == 0 and colour:
+                for i, yy in enumerate(order):
+                    if colour == 1:
+                        for d, step in enumerate((1, -1)):
+                            k = i * 2 + d
+                            self.split.append(
+                                remote(
+                                    self.buf.at[((self.mine + 2) % 4,) + self.halves[d] + (yy,)],
+                                    self.far[d].at[pl.ds(0, 2), yy],
+                                    far_send.at[k],
+                                    far_recv.at[k],
+                                    neighbour(self.axis, step),
+                                )
+                            )
+                    else:
+                        k = 8 + i
+                        d = yy // 2
+                        self.split.append(
+                            remote(
+                                self.buf.at[(self.mine + 2) % 4, yy],
+                                fars[colour][0].at[d, yy % 2],
+                                far_send.at[k],
+                                far_recv.at[k],
+                                neighbour(self.axis, 1 - 2 * d),
+                            )
+                        )
+
         def add(self, target, parts):
             if self.phase == 0:
                 add_into(target, parts)
@@ -305,14 +362,22 @@
             for d in range(2):
                 self.copies[d][0].start()
 
+        def far_part(self, i):
+            n = len(self.split) // 4
+            for c in self.split[i * n : i * n + n]:
+                c.start()
+
         def own_out(self):
             for d in range(2):
                 self.copies[d][1].start()
 
         def middle(self):
+            for c in self.split:
+                c.wait_recv()
             for d in range(2):
                 far, _, onward, acc = self.copies[d]
-                far.wait_recv()
+                if not self.split:
+                    far.wait_recv()
                 self.add(acc, [self.far[d]])
                 onward.start()
 
@@ -323,8 +388,10 @@
             self.add(self.buf.at[self.mine], self.near)
 
         def drain(self):
-            for d in range(2):
-                for c in range(3):
+            for c in self.split:
+                c.wait_send()
+            for d in range(2):
+                for c in range(1 if self.split else 0, 3):
                     self.copies[d][c].wait_send()
 
     class Turn:
@@ -401,55 +468,76 @@
 
     def unpack():
         lined.wait_recv()
-        table[...] = arrived[...].reshape(2048, 128).astype(f32)
-        marks, before = [], 0.0
-        for place in range(2):
-            mark = table[pl.ds(place * 8 + 6, 128, stride=16), :][:, 6:7]
-            marks.append(jnp.sum(jnp.where(row == col, mark, 0.0), axis=0, keepdims=True))
-            before = before + jnp.sum(jnp.where(row < col, mark, 0.0), axis=0, keepdims=True)
-        target = jnp.concatenate([before, before + marks[0]], axis=1)
-        mark = jnp.concatenate(marks, axis=1)
+        seconds_lined.wait_recv()
+        table[...] = arrived[...].reshape(1024, 128).astype(f32)
+        side = table[pl.ds(6, 128, stride=8), :]
+        mark = jnp.sum(jnp.where(row == col, side[:, 6:7], 0.0), axis=0, keepdims=True)
+        counted = jnp.sum(jnp.where(row == col, side[:, 7:8], 0.0), axis=0, keepdims=True)
+        before = jnp.sum(jnp.where(row < col, side[:, 7:8], 0.0), axis=0, keepdims=True)
+        after = jnp.sum(jnp.where(counted > 1.5, before + 1.0, 0.0), axis=1, keepdims=True)
+        tile = second_last[0].astype(f32)
+        for n in range(1, 8):
+            tile = tile + second_last[n].astype(f32)
         blocks = jnp.concatenate(
-            [
-                jnp.concatenate(
-                    [table[pl.ds(place * 8 + q, 128, stride=16), :].astype(b16) for q in range(7)],
-                    axis=1,
-                )
-                for place in range(2)
-            ],
-            axis=0,
+            [table[pl.ds(q, 128, stride=8), :].astype(b16) for q in range(7)], axis=1
         )
-        new_row = lax.broadcasted_iota(jnp.int32, (64, 256), 0).astype(f32)
+        new_row = row[0:64].astype(f32)
         for h in range(2):
-            choose = (target == 2.0 * new_row + h) & (mark > 0.5)
-            owned[h] = jnp.dot(
+            choose = (before == 2.0 * new_row + h) & (mark > 0.5)
+            got = jnp.dot(
                 jnp.where(choose, 1.0, 0.0).astype(b16), blocks, preferred_element_type=f32
             )
+            here_too = 2.0 * new_row + h == after
+            for q in range(7):
+                cols = slice(q * 128, q * 128 + 128)
+                owned[h, :, cols] = got[:, cols] + jnp.where(here_too, tile[q : q + 1, :], 0.0)
             whole[y, core, z, x, :, h * 256 : h * 256 + 256] = owned[h, :, 0:256].astype(b16)
-
 
     own_part(2)
     own_part(3)
     dealt.wait_recv()
+    seconds.wait_recv()
     arrived[cut] = middle[cut]
+    held = [second_out[n].astype(f32) for n in range(16)]
+    for c in range(8):
+        wanted = (fs + c * 16).astype(f32)
+        tile = jnp.zeros((8, 128), f32)
+        for n in range(16):
+            tile = tile + jnp.where(held[n][6:7, 7:8] == wanted, held[n], 0.0)
+        second_mid[c] = tile.astype(b16)
+    second_last[cut] = second_mid[cut]
     for s in range(1, 8):
         other = (cut + s) % 8
         remote(middle.at[other], arrived.at[cut], line_send, line_recv, (other, fs)).start()
+        remote(
+            second_mid.at[other], second_last.at[cut], extra_line_send, extra_line_recv, (other, fs)
+        ).start()
     lined = remote(
         middle.at[pl.ds(0, 7)], arrived.at[pl.ds(0, 7)], line_send, line_recv, partner
+    )
+    seconds_lined = remote(
+        second_mid.at[pl.ds(0, 7)],
+        second_last.at[pl.ds(0, 7)],
+        extra_line_send,
+        extra_line_recv,
+        partner,
     )
     pairs[0].wait_recv()
     pair_part(0)
     each(stages[0][:1], "far_out")
+    each(stages[0][1:], "far_part", 0)
     pair_part(1)
+    each(stages[0][1:], "far_part", 1)
     pair_part(2)
+    each(stages[0][1:], "far_part", 2)
+    each(stages[0][:1], "own_out")
     pair_part(3)
-    each(stages[0][1:], "far_out")
+    each(stages[0][1:], "far_part", 3)
+    each(stages[0][1:], "own_out")
     unpack()
     each(turns[0], "begin")
-    each(stages[0], "own_out")
+    each(stages[0], "middle")
     each(turns[0], "middle")
-    each(stages[0], "middle")
     each(turns[0], "finish")
     each(turns[1], "begin")
     each(stages[0], "finish")
@@ -562,6 +650,8 @@
     for c in pairs:
         c.wait_send()
     lined.wait_send()
+    seconds.wait_send()
+    seconds_lined.wait_send()
     dealt.wait_send()
     for group in stages + turns:
         each(group, "drain")
@@ -597,10 +687,13 @@
         pltpu.VMEM((256, 128), f32),
         pltpu.VMEM((16, 8, 128), f32),
         pltpu.VMEM((8, 8, 128), f32),
-        pltpu.VMEM((2048, 128), f32),
-        pltpu.VMEM((8, 16, 16, 128), b16),
-        pltpu.VMEM((8, 16, 16, 128), b16),
-        pltpu.VMEM((8, 16, 16, 128), b16),
+        pltpu.VMEM((1024, 128), f32),
+        pltpu.VMEM((8, 16, 8, 128), b16),
+        pltpu.VMEM((8, 16, 8, 128), b16),
+        pltpu.VMEM((8, 16, 8, 128), b16),
+        pltpu.VMEM((16, 8, 128), b16),
+        pltpu.VMEM((8, 8, 128), b16),
+        pltpu.VMEM((8, 8, 128), b16),
         pltpu.VMEM((2, 64, 896), f32),
         pltpu.VMEM((128, 256), b16),
         pltpu.VMEM((128, 256), b16),
@@ -613,8 +706,14 @@
         pltpu.SemaphoreType.DMA((5,)),
         pltpu.SemaphoreType.DMA((54,)),
         pltpu.SemaphoreType.DMA((54,)),
+        pltpu.SemaphoreType.DMA((12,)),
+        pltpu.SemaphoreType.DMA((12,)),
         pltpu.SemaphoreType.DMA((24,)),
         pltpu.SemaphoreType.DMA((24,)),
+        pltpu.SemaphoreType.DMA,
+        pltpu.SemaphoreType.DMA,
+        pltpu.SemaphoreType.DMA,
+        pltpu.SemaphoreType.DMA,
         pltpu.SemaphoreType.DMA,
         pltpu.SemaphoreType.DMA,
         pltpu.SemaphoreType.DMA,

time: 88.9 us -> 85.4 us (0.961)
  Pallas kernels: 88 us -> 84.5 us
    pallas_call x1, Pallas kernels: 81.7 us -> 78.2 us  [main_call(): pl.pallas_call(main_kernel, out_shape=(pltpu.VMEM((4, 2, 4, 4, 64, 512),...]
where the time goes in v1:
time: 85.4 us; the launch traced here: 85.3 us
  Pallas kernels  84.5 us (99%)
    pallas_call x1, Pallas kernels, main_call(): pl.pallas_call(main_kernel, out_shape=(pltpu.VMEM((4, 2, 4, 4, 64, 512),...  78.2 us
    pallas_call x1, Pallas kernels, last_call(): pl.pallas_call(last_kernel, out_shape=[jax.ShapeDtypeStruct((512, 8192),...  6.28 us

profile of v1, /device:TPU:1, one launch (start us, length us, event | category | flops | bytes accessed | tf_op | source)
XLA Modules:
  0.0 85.3 jit_solution(9562925853313495565)
XLA Ops:
  0.6 78.2 %exchange_adam.1 = (bf16[4,2,4,4,64,512]{5,4,3,2,1,0:T(8,128)(2,1)S(1)}, bf16[512,512]{1,0:T(8,128)(2,1)S(1)}, bf16[64,512]{1,0:T(8,128)(2,1)S(1)}, bf16[64,512]...) custom-call(bf16[512,8192]{1,0:T(8,128)(2,1)} %hidden.1, ...), custom_call_target="tpu_custom_call" | custom-call | tf_op jit(solution)/shard_map/exchange_adam/pallas_call | solution.py:726
  78.8 6.3 %input_grad.1 = (bf16[512,8192]{1,0:T(8,128)(2,1)}, bf16[64,512]{1,0:T(8,128)(2,1)}, bf16[64,512]{1,0:T(8,128)(2,1)}, f32[2,64]{1,0:T(2,128)}, bf16[64,512]{1,0:T(8,128)(2,1)}, /*index=5*/f32[2,64]{1,0:T(2,128)}) custom-call(bf16[512,512]{1,0:T(8,128)(2,1)S(1)} %get-tuple-element.19.cotangent, bf16[4,2,4,4,64,512]{5,4,3,2,1,0:T(8,128)(2,1)S(1)} %get-tuple-element.20.weight, ...), custom_call_target="tpu_custom_call" | custom-call | tf_op jit(solution)/shard_map/input_grad/pallas_call | solution.py:774

commit v2 on v1

--- a/solution.py
+++ b/solution.py
@@ -546,10 +546,10 @@
     each(turns[1], "middle")
     each(stages[1], "middle")
     each(turns[1], "finish")
-    each(turns[2], "begin", 0)
     passes = [hand(t, t.mine, 0) for t in turns[2]]
     for p in passes:
         p.start()
+    each(turns[2], "begin", 0)
     each(stages[1], "finish")
     each(stages[2], "far_out")
     each(stages[2], "own_out")
@@ -557,6 +557,7 @@
     each(turns[2], "middle", 0)
     each(stages[2], "middle")
     each(turns[2], "begin", 2)
+    each(turns[2], "begin", 3)
     each(stages[2], "finish")
 
     for colour in range(3):
@@ -587,7 +588,6 @@
 
     plane[fs] = squares
     told = tell(plane, fs, 16, 0, lambda s: (cut, (fs + s) % 16))
-    each(turns[2], "begin", 3)
     each(turns[2], "middle", 1)
     for t in turns[2]:
         t.arrive(2)

time: 85.4 us -> 84.4 us (0.988)
  Pallas kernels: 84.5 us -> 83.5 us
    pallas_call x1, Pallas kernels: 78.2 us -> 77.2 us  [main_call(): pl.pallas_call(main_kernel, out_shape=(pltpu.VMEM((4, 2, 4, 4, 64, 512),...]
where the time goes in v2:
time: 84.4 us; the launch traced here: 84.3 us
  Pallas kernels  83.5 us (99%)
    pallas_call x1, Pallas kernels, main_call(): pl.pallas_call(main_kernel, out_shape=(pltpu.VMEM((4, 2, 4, 4, 64, 512),...  77.2 us
    pallas_call x1, Pallas kernels, last_call(): pl.pallas_call(last_kernel, out_shape=[jax.ShapeDtypeStruct((512, 8192),...  6.28 us

profile of v2, /device:TPU:1, one launch (start us, length us, event | category | flops | bytes accessed | tf_op | source)
XLA Modules:
  0.0 84.3 jit_solution(1210758379998563976)
XLA Ops:
  0.6 77.2 %exchange_adam.1 = (bf16[4,2,4,4,64,512]{5,4,3,2,1,0:T(8,128)(2,1)S(1)}, bf16[512,512]{1,0:T(8,128)(2,1)S(1)}, bf16[64,512]{1,0:T(8,128)(2,1)S(1)}, bf16[64,512]...) custom-call(bf16[512,8192]{1,0:T(8,128)(2,1)} %hidden.1, ...), custom_call_target="tpu_custom_call" | custom-call | tf_op jit(solution)/shard_map/exchange_adam/pallas_call | solution.py:726
  77.9 6.3 %input_grad.1 = (bf16[512,8192]{1,0:T(8,128)(2,1)}, bf16[64,512]{1,0:T(8,128)(2,1)}, bf16[64,512]{1,0:T(8,128)(2,1)}, f32[2,64]{1,0:T(2,128)}, bf16[64,512]{1,0:T(8,128)(2,1)}, /*index=5*/f32[2,64]{1,0:T(2,128)}) custom-call(bf16[512,512]{1,0:T(8,128)(2,1)S(1)} %get-tuple-element.19.cotangent, bf16[4,2,4,4,64,512]{5,4,3,2,1,0:T(8,128)(2,1)S(1)} %get-tuple-element.20.weight, ...), custom_call_target="tpu_custom_call" | custom-call | tf_op jit(solution)/shard_map/input_grad/pallas_call | solution.py:774
